TPU v7x, 32 devices: a whole 2x2x4 slice. The times are simulated.
32 devices in a mesh: groups: 2 (over y), samples: 8 (over z, x), genome: 2 (over core).
Axes of the slice: x: 2, y: 2, z: 4, core: 2. Of those that a mesh axis runs over, the one named last changes fastest.
Arguments:
- genotypes: bfloat16 [16384, 1536], P(('groups', 'samples'), 'genome'), parts along dimension 0, may hold values from 0 to 2
- chromosome: int32 [3072], P('groups'), parts along dimension 0, may hold values from 1 to 3, as said below
- blocks: int32 [3072], P('groups'), parts along dimension 0, may hold values from 0 to 199, never falling along the last dimension, each value on 1 to 16 neighbouring positions
- annotation: int32 [97, 3072], P(None, 'groups'), parts along dimension 1, may hold values 0 or 1
- reach: int32 [3072], P('groups'), parts along dimension 0, may hold values from 384 to 768
Outputs:
- ld_scores: float32 [97, 3072], P(None, ('groups', 'genome')), parts along dimension 1
- block_sums: float32 [97, 400], P(None, 'groups'), parts along dimension 1
There are 2 independent parts, one for each index of `groups`. A program takes and returns all parts, laid end to end along the dimension named above; each array names one. Nothing has to cross between parts.
Inputs may be any that keep to these rules, and one draw needn't show every extreme that they name: chromosome ids never fall along the window and rise by one at each of 2 boundaries.
All inputs are finite; a program needn't handle non-finite values.
Results may differ from a plain program's by a relative error of at most 0.0015.
Values may be sent and summed in bfloat16 or wider, within the bound.
No kernel may reach another device: no remote copies, remote signals or barrier semaphores. Data moves between devices by JAX's collectives and lax.ppermute only.
A program may use at most 64 MiB of HBM per device.

v0:
```python
import jax
import jax.numpy as jnp
from jax import lax
from jax.sharding import PartitionSpec as P

BAND = 768
NBLK = 200
VAR_EPS = 1e-06


def shifted(block, axis, distance):
    devices = range(lax.axis_size(axis))
    route = [(i - distance, i) for i in devices if i - distance in devices]
    return lax.ppermute(block, axis, route)


def shear_band(product, band_len):
    rows_here, columns = product.shape
    flattened = jnp.pad(product.reshape(-1), (0, rows_here))
    return flattened.reshape(rows_here, columns + 1)[:, :band_len]


def unshear_band(gram_band):
    rows_here, band_len = gram_band.shape
    col_span = rows_here + band_len
    padded = jnp.pad(gram_band, ((0, 0), (1, rows_here)))
    return padded.reshape(-1)[: rows_here * col_span].reshape(rows_here, col_span)


def gram_rows(extended, row_start, row_count, band_len):
    left_cols = lax.dynamic_slice_in_dim(extended, row_start, row_count, 1)
    right_cols = lax.dynamic_slice_in_dim(extended, row_start + 1, row_count + band_len - 1, 1)
    product = lax.dot_general(
        left_cols, right_cols, (((0,), (0,)), ((), ())), preferred_element_type=jnp.float32
    )
    return shear_band(product, band_len)


def score_terms(
    gram_band,
    row_start,
    col_means,
    scales,
    chrom_ext,
    reach_own,
    annot_ext,
    first_col,
    snp_total,
    samples_all,
):
    row_count, band_len = gram_band.shape
    col_span = row_count + band_len
    dense_band = unshear_band(gram_band)
    mean_rows = lax.dynamic_slice_in_dim(col_means, row_start, row_count)
    scale_rows = lax.dynamic_slice_in_dim(scales, row_start, row_count)
    chrom_rows = lax.dynamic_slice_in_dim(chrom_ext, row_start, row_count)
    correl = (dense_band / samples_all - mean_rows[:, None] * col_means[None, :]) / (
        scale_rows[:, None] * scales[None, :]
    )
    squared = correl * correl
    unbiased = squared - (1.0 - squared) / (samples_all - 2.0)
    offsets = jnp.arange(col_span)[None, :] - jnp.arange(row_count)[:, None]
    col_index = first_col + row_start + jnp.arange(col_span)
    allowed = (
        (offsets >= 1)
        & (offsets <= reach_own[:, None])
        & (col_index[None, :] < snp_total)
        & (chrom_rows[:, None] == chrom_ext[None, :])
    )
    weights = jnp.where(allowed, unbiased, 0.0)
    annot_rows = lax.dynamic_slice_in_dim(annot_ext, row_start, row_count, 1)
    forward = lax.dot_general(
        annot_ext, weights, (((1,), (1,)), ((), ())), precision=lax.Precision.HIGHEST
    )
    backward = jnp.dot(annot_rows, weights, precision=lax.Precision.HIGHEST)
    empty_scores = jnp.zeros(annot_ext.shape, jnp.float32)
    placed_fore = lax.dynamic_update_slice_in_dim(empty_scores, forward, row_start, 1)
    return backward + placed_fore


def body(genotypes, chromosome, blocks, annotation, reach):
    slab_len = genotypes.shape[1]
    band_len = BAND
    snp_total = chromosome.shape[0]
    samples_all = float(genotypes.shape[0] * lax.axis_size("samples"))
    first_col = lax.axis_index("genome") * slab_len
    next_cols = shifted(genotypes, "genome", -1)
    extended = jnp.concatenate([genotypes, next_cols], axis=1)
    ext_values = extended.astype(jnp.float32)
    col_sums, squares = lax.psum(
        (jnp.sum(ext_values, 0), jnp.sum(ext_values * ext_values, 0)), "samples"
    )
    col_means = col_sums / samples_all
    variance = squares / samples_all - col_means * col_means + VAR_EPS
    scales = jnp.sqrt(variance)
    chrom_pad = jnp.pad(chromosome, (0, band_len), constant_values=-1)
    chrom_ext = lax.dynamic_slice_in_dim(chrom_pad, first_col, slab_len + band_len)
    reach_own = lax.dynamic_slice_in_dim(reach, first_col, slab_len)
    annot_pad = jnp.pad(annotation.astype(jnp.float32), ((0, 0), (0, band_len)))
    annot_ext = lax.dynamic_slice_in_dim(annot_pad, first_col, slab_len + band_len, 1)
    gram_band = lax.psum(gram_rows(extended, 0, slab_len, band_len), "samples")
    scores = score_terms(
        gram_band,
        0,
        col_means,
        scales,
        chrom_ext,
        reach_own,
        annot_ext,
        first_col,
        snp_total,
        samples_all,
    )
    carried = shifted(scores[:, slab_len:].astype(jnp.bfloat16), "genome", 1).astype(jnp.float32)
    ld_scores = annot_ext[:, :slab_len] + scores[:, :slab_len] + carried
    block_own = lax.dynamic_slice_in_dim(blocks, first_col, slab_len)
    onehot = (block_own[None, :] == jnp.arange(NBLK)[:, None]).astype(jnp.float32)
    block_part = lax.dot_general(
        ld_scores, onehot, (((1,), (1,)), ((), ())), precision=lax.Precision.HIGHEST
    )
    block_sums = lax.psum(block_part, "genome")
    return (ld_scores, block_sums)


def solution(mesh):
    placed = (
        P(("groups", "samples"), "genome"),
        P("groups"),
        P("groups"),
        P(None, "groups"),
        P("groups"),
    )
    return jax.shard_map(
        body,
        mesh=mesh,
        in_specs=placed,
        out_specs=(P(None, ("groups", "genome")), P(None, "groups")),
        check_vma=False,
    )
```

profile of v0, /device:TPU:0, one launch (start us, length us, event | category | flops | bytes accessed | tf_op | source)
XLA Modules:
  0.0 224.0 jit_solution(105049170321501688)
XLA Ops:
  7.2 0.0 copy-start.1
  7.2 0.0 all-reduce.9.cloned.1.call-start
  7.2 1.4 collective-permute-start
  8.7 1.5 constant_dynamic-update-slice_fusion.1
  10.2 2.7 %collective-permute-done = bf16[1024,768]{1,0:T(8,128)(2,1)S(1)} collective-permute-done((bf16[1024,768]{1,0:T(8,128)(2,1)}, bf16[1024,768]{1,0:T(8,128)(2,1)S(1)}, u32[]{:S(2)}, u32[]{:S(2)}) %collective-permute-start) | collective-permute-done | bytes 1572896 | tf_op jit(solution)/shard_map/ppermute | solution.py:14
  12.9 0.1 constant_dynamic-update-slice_fusion
  13.0 0.0 copy-start
  13.0 1.6 copy-done
  14.6 0.0 copy-done.1
  14.6 4.9 %convolution_bitcast_fusion = f32[768,1535]{0,1:T(8,128)} fusion(bf16[1024,768]{1,0:T(8,128)(2,1)S(1)} %copy-done.1, bf16[1024,1536]{1,0:T(8,128)(2,1)S(1)} %constant_dynamic-update-slice_fusion), kind=kOutput, calls=%fused_computation.11 | convolution fusion | flops 2414346240 | bytes 9434112 | tf_op jit(solution)/shard_map/dot_general | solution.py:33
  19.6 6.1 %copy.7 = f32[768,1535]{1,0:T(8,128)} copy(f32[768,1535]{0,1:T(8,128)} %convolution_bitcast_fusion) | data formatting | bytes 9431040 | tf_op jit(solution)/shard_map/dot_general | solution.py:33
  25.6 7.8 %reshape.30 = f32[1178880]{0:T(1024)} reshape(f32[768,1535]{1,0:T(8,128)} %copy.7) | data formatting | bytes 9431040 | tf_op jit(solution)/shard_map/reshape | solution.py:19
  33.5 4.1 %pad.19 = f32[1179648]{0:T(1024)} pad(f32[1178880]{0:T(1024)} %reshape.30, f32[]{:T(128)} %constant.12.clone.1), padding=0_768 | pad | bytes 9434116 | tf_op jit(solution)/shard_map/jit(_pad)/pad | solution.py:19
  37.6 5.8 %reshape.31 = f32[768,1536]{1,0:T(8,128)} reshape(f32[1179648]{0:T(1024)} %pad.19) | data formatting | bytes 9437184 | tf_op jit(solution)/shard_map/reshape | solution.py:20
  43.4 0.0 copy-start.3
  43.4 0.0 copy-start.5
  43.4 0.0 copy-start.4
  43.4 3.3 %slice.21 = f32[768,768]{1,0:T(8,128)} slice(f32[768,1536]{1,0:T(8,128)} %reshape.31), slice={[0:768], [0:768]} | slice | bytes 4718592 | tf_op jit(solution)/shard_map/slice | solution.py:20
  46.7 0.0 all-reduce.9.cloned.1.call-update
  46.7 0.0 all-reduce.11.cloned.1.call-start
  46.8 0.0 copy-done.3
  46.8 0.0 copy-done.5
  46.8 0.1 dynamic_slice.26
  46.9 0.0 copy-done.4
  46.9 0.1 pad_dynamic-slice_fusion.4
  47.0 0.1 pad_dynamic-slice_fusion.5
  47.1 2.8 %convert_reduce_fusion = (f32[1536]{0:T(1024)S(1)}, f32[1536]{0:T(1024)S(1)}) fusion(bf16[1024,1536]{1,0:T(8,128)(2,1)} %copy-done), kind=kLoop, calls=%fused_computation.1 | loop fusion | flops 6288384 | bytes 3158016 | tf_op jit(solution)/shard_map/reduce_sum | solution.py:91
  49.9 40.4 %all-reduce.5 = (f32[1536]{0:T(1024)S(1)}, f32[1536]{0:T(1024)S(1)}) all-reduce(f32[1536]{0:T(1024)S(1)} %get-tuple-element.3, f32[1536]{0:T(1024)S(1)} %get-tuple-element.2), channel_id=1, replica_groups=mesh['groups'=2,'samples'=8,'genome'=2] {'samples'}, use_global_device_ids=true, to_apply=%region_4.5 | all-reduce | flops 3072 | bytes 24576 | tf_op jit(solution)/shard_map/psum | solution.py:90
  90.2 68.6 %all-reduce.9.cloned.1.call-done = f32[768,768]{1,0:T(8,128)} async-done(((f32[768,768]{1,0:T(8,128)}), f32[768,768]{1,0:T(8,128)}) %all-reduce.9.cloned.1.call-update) | async-done | bytes 2359312 | tf_op jit(solution)/shard_map/psum | solution.py:101
  158.9 4.8 %pad.20 = f32[768,1537]{1,0:T(8,128)} pad(f32[768,768]{1,0:T(8,128)} %all-reduce.9.cloned.1.call-done, f32[]{:T(128)} %constant.12.clone.1), padding=0_0x1_768 | pad | bytes 7080964 | tf_op jit(solution)/shard_map/jit(_pad)/pad | solution.py:26
  163.7 8.1 %reshape.32 = f32[1180416]{0:T(1024)} reshape(f32[768,1537]{1,0:T(8,128)} %pad.20) | data formatting | bytes 9443328 | tf_op jit(solution)/shard_map/reshape | solution.py:27
  171.8 3.9 %slice_multiply_fusion = f32[1179648]{0:T(1024)} fusion(f32[1180416]{0:T(1024)} %reshape.32), kind=kLoop, calls=%fused_computation.3 | loop fusion | flops 1179648 | bytes 9437184 | tf_op jit(solution)/shard_map/div | solution.py:57
  175.8 5.8 %div.25 = f32[768,1536]{1,0:T(8,128)} reshape(f32[1179648]{0:T(1024)} %slice_multiply_fusion) | data formatting | bytes 9437184 | tf_op jit(solution)/shard_map/div | solution.py:57
  181.6 5.4 %subtract_select_fusion = f32[768,1536]{1,0:T(8,128)S(1)} fusion(f32[768,1536]{1,0:T(8,128)} %div.25, f32[1536]{0:T(1024)S(1)} %get-tuple-element.7, f32[768]{0:T(1024)S(1)} %dynamic_slice.35, f32[1536]{0:T(1024)S(1)} %get-tuple-element.6, f32[768]{0:T(1024)S(1)} %dynamic_slice.34, s32[1536]{0:T(1024)S(1)} %pad_dynamic-slice_fusion.5, ...), kind=kLoop, calls=%fused_computation.4 | loop fusion | flops 18874368 | bytes 9469440 | tf_op jit(solution)/shard_map/jit(_where)/select_n | solution.py:70
  187.0 4.7 %fusion.7 = f32[97,768]{1,0:T(8,128)S(1)} fusion(f32[768,1536]{1,0:T(8,128)S(1)} %subtract_select_fusion, s32[]{:T(128)S(6)} %select_n.12, f32[97,1536]{1,0:T(8,128)S(1)} %convert_element_type.17), kind=kOutput, calls=%fused_computation.16 | convolution fusion | flops 1373110272 | bytes 5612548 | tf_op jit(solution)/shard_map/dot_general | solution.py:72
  191.7 0.0 copy-start.6
  191.7 2.7 %convolution_add_fusion = f32[97,1536]{1,0:T(8,128)S(1)} fusion(f32[768,1536]{1,0:T(8,128)S(1)} %subtract_select_fusion, f32[97,768]{1,0:T(8,128)S(1)} %fusion.7, s32[]{:T(128)S(6)} %select_n.12, f32[97,1536]{1,0:T(8,128)S(1)} %convert_element_type.17), kind=kOutput, calls=%fused_computation.13 | convolution fusion | flops 1373259264 | bytes 6208516 | tf_op jit(solution)/shard_map/dot_general | solution.py:75
  194.5 1.3 collective-permute-start.1
  195.8 0.0 copy-done.6
  195.8 0.1 dynamic_slice.32
  195.9 0.9 collective-permute-done.1
  196.8 0.1 fusion.9
  196.9 0.0 copy-start.2
  196.9 1.1 fusion.8
  198.0 0.0 all-reduce.11.cloned.1.call-update
  198.0 17.6 %all-reduce.11.cloned.1.call-done = f32[97,200]{0,1:T(8,128)} async-done(((f32[97,200]{0,1:T(8,128)}), f32[97,200]{0,1:T(8,128)}) %all-reduce.11.cloned.1.call-update) | async-done | bytes 77616 | tf_op jit(solution)/shard_map/psum | solution.py:121
  215.6 1.5 copy.11
  217.1 0.0 copy-done.2
  (6 shorter events, 0.1 us)
Async XLA Ops:
  7.2 7.5 %copy-start.1 = (bf16[1024,768]{1,0:T(8,128)(2,1)S(1)}, bf16[1024,768]{1,0:T(8,128)(2,1)}, u32[]{:S(2)}) copy-start(bf16[1024,768]{1,0:T(8,128)(2,1)} %param.5) | copy-start | bytes 4718596
  7.2 151.7 %all-reduce.9.cloned.1.call-start = ((), (), s32[]{:S(2)}) async-start(), calls=%async_computation | async-start | bytes 4718592 | tf_op jit(solution)/shard_map/psum | solution.py:101
  7.2 5.6 %collective-permute-start = (bf16[1024,768]{1,0:T(8,128)(2,1)}, bf16[1024,768]{1,0:T(8,128)(2,1)S(1)}, u32[]{:S(2)}, u32[]{:S(2)}) collective-permute-start(bf16[1024,768]{1,0:T(8,128)(2,1)} %param.5), channel_id=1, source_target_pairs={{1,0},{3,2},{5,4},{7,6},{9,8},{11,10},{13,12},{15,14},{17,16},{19,... | collective-permute-start | bytes 4718600 | tf_op jit(solution)/shard_map/ppermute | solution.py:14
  13.0 1.6 copy-start
  43.4 3.4 %copy-start.3 = (s32[97,1536]{1,0:T(8,128)S(1)}, s32[97,1536]{1,0:T(8,128)}, u32[]{:S(2)}) copy-start(s32[97,1536]{1,0:T(8,128)} %param.8) | copy-start | bytes 1787908
  43.4 3.5 %copy-start.5 = (s32[1536]{0:T(1024)S(1)}, s32[1536]{0:T(1024)}, u32[]{:S(2)}) copy-start(s32[1536]{0:T(1024)} %param.9) | copy-start | bytes 18436
  43.4 3.6 %copy-start.4 = (s32[1536]{0:T(1024)S(1)}, s32[1536]{0:T(1024)}, u32[]{:S(2)}) copy-start(s32[1536]{0:T(1024)} %param.6) | copy-start | bytes 18436
  46.7 168.9 %all-reduce.11.cloned.1.call-start = ((), (), s32[]{:S(2)}) async-start(), calls=%async_computation.1 | async-start | bytes 204800 | tf_op jit(solution)/shard_map/psum | solution.py:121
  191.7 4.1 %copy-start.6 = (s32[1536]{0:T(1024)S(1)}, s32[1536]{0:T(1024)}, u32[]{:S(2)}) copy-start(s32[1536]{0:T(1024)} %param.7) | copy-start | bytes 18436
  194.5 2.3 %collective-permute-start.1 = (bf16[97,768]{1,0:T(8,128)(2,1)S(1)}, bf16[97,768]{1,0:T(8,128)(2,1)S(1)}, u32[]{:S(2)}, u32[]{:S(2)}) collective-permute-start(bf16[97,768]{1,0:T(8,128)(2,1)S(1)} %slice.30), channel_id=1, source_target_pairs={{0,1},{2,3},{4,5},{6,7},{8,9},{10,11},{12,13},{14,15},{16,17},{18,... | collective-permute-start | bytes 446984 | tf_op jit(solution)/shard_map/ppermute | solution.py:14
  196.9 20.3 %copy-start.2 = (f32[97,768]{1,0:T(8,128)}, f32[97,768]{1,0:T(8,128)S(1)}, u32[]{:S(2)}) copy-start(f32[97,768]{1,0:T(8,128)S(1)} %fusion.9) | copy-start | bytes 893956
Sparse Core Ops, SparseCore 0:
  46.8 112.0 all-reduce.8
  198.1 17.4 all-reduce.10
where the time goes:
time: 225 us; the launch traced here: 224 us
  waiting for transfers between devices  89.8 us (40%)
  local copies, waits for them, and re-layouts  51 us (23%)
  blocking collectives  40.4 us (18%)
  between operations  14.2 us (6%)
  matrix products  13.5 us (6%)
  other arithmetic  12.3 us (5%)
  starting transfers between devices  2.8 us (1%)
    psum x1, waiting for transfers between devices, body(): gram_band = lax.psum(gram_rows(extended, 0, slab_len, band_len), 'samples')  68.6 us
    psum x1, blocking collectives, body(): lax.psum((jnp.sum(ext_values, 0), jnp.sum(ext_values * ext_values, 0)), '...  40.4 us
    psum x1, waiting for transfers between devices, body(): block_sums = lax.psum(block_part, 'genome')  17.6 us
    reshape x1, local copies, waits for them, and re-layouts, unshear_band(): padded.reshape(-1)[:rows_here * col_span].reshape(rows_here, col_span)  8.14 us
    reshape x1, local copies, waits for them, and re-layouts, shear_band(): flattened = jnp.pad(product.reshape(-1), (0, rows_here))  7.84 us
    dot_general x1, local copies, waits for them, and re-layouts, gram_rows(): lax.dot_general(left_cols, right_cols, (((0,), (0,)), ((), ())), preferre...  6.05 us
    reshape x1, local copies, waits for them, and re-layouts, shear_band(): return flattened.reshape(rows_here, columns + 1)[:, :band_len]  5.81 us
    div x1, local copies, waits for them, and re-layouts, score_terms(): dense_band / samples_all - mean_rows[:, None] * col_means[None, :]  5.81 us
  transfers between devices with their start and end apart: 4, of which 4 were waited for; matrix products, arithmetic and copies ran while one was open for 2% of the time, Pallas kernels for 0%

commit v1 on v0

--- a/solution.py
+++ b/solution.py
@@ -118,7 +118,8 @@
     block_part = lax.dot_general(
         ld_scores, onehot, (((1,), (1,)), ((), ())), precision=lax.Precision.HIGHEST
     )
-    block_sums = lax.psum(block_part, "genome")
+    parts = lax.all_gather(block_part, "genome")
+    block_sums = jnp.sum(parts, axis=0)
     return (ld_scores, block_sums)
 
 

time: 225 us -> 208 us (0.924)
  waiting for transfers between devices: 89.8 us -> 72.3 us
    psum x1 -> x0, waiting for transfers between devices: 17.6 us -> none  [body(): block_sums = lax.psum(block_part, 'genome')]
    unnamed x16 -> x15, local copies, waits for them, and re-layouts: 4.72 us -> 3.18 us
  transfers between devices with their start and end apart: 4 -> 3, of which waited for: 4 -> 3; matrix products, arithmetic and copies ran while one was open for 2% -> 2% of each run, Pallas kernels for 0% -> 0%
where the time goes in v1:
time: 208 us; the launch traced here: 207 us
  waiting for transfers between devices  72.3 us (35%)
  local copies, waits for them, and re-layouts  49.5 us (24%)
  blocking collectives  42.3 us (20%)
  between operations  14.2 us (7%)
  other arithmetic  12.9 us (6%)
  matrix products  12.8 us (6%)
  starting transfers between devices  2.76 us (1%)
    psum x1, waiting for transfers between devices, body(): gram_band = lax.psum(gram_rows(extended, 0, slab_len, band_len), 'samples')  68.7 us
    psum x1, blocking collectives, body(): lax.psum((jnp.sum(ext_values, 0), jnp.sum(ext_values * ext_values, 0)), '...  40.4 us
    reshape x1, local copies, waits for them, and re-layouts, unshear_band(): padded.reshape(-1)[:rows_here * col_span].reshape(rows_here, col_span)  8.14 us
    reshape x1, local copies, waits for them, and re-layouts, shear_band(): flattened = jnp.pad(product.reshape(-1), (0, rows_here))  7.83 us
    dot_general x1, local copies, waits for them, and re-layouts, gram_rows(): lax.dot_general(left_cols, right_cols, (((0,), (0,)), ((), ())), preferre...  6.05 us
    reshape x1, local copies, waits for them, and re-layouts, shear_band(): return flattened.reshape(rows_here, columns + 1)[:, :band_len]  5.83 us
    div x1, local copies, waits for them, and re-layouts, score_terms(): dense_band / samples_all - mean_rows[:, None] * col_means[None, :]  5.83 us
    select_n x1, other arithmetic, score_terms(): weights = jnp.where(allowed, unbiased, 0.0)  5.45 us
  transfers between devices with their start and end apart: 3, of which 3 were waited for; matrix products, arithmetic and copies ran while one was open for 2% of the time, Pallas kernels for 0%

profile of v1, /device:TPU:0, one launch (start us, length us, event | category | flops | bytes accessed | tf_op | source)
XLA Modules:
  0.0 206.9 jit_solution(8248477015087986288)
XLA Ops:
  7.2 0.0 copy-start.1
  7.2 0.0 all-reduce.8.cloned.1.call-start
  7.2 1.4 collective-permute-start
  8.7 1.5 constant_dynamic-update-slice_fusion.1
  10.2 2.7 %collective-permute-done = bf16[1024,768]{1,0:T(8,128)(2,1)S(1)} collective-permute-done((bf16[1024,768]{1,0:T(8,128)(2,1)}, bf16[1024,768]{1,0:T(8,128)(2,1)S(1)}, u32[]{:S(2)}, u32[]{:S(2)}) %collective-permute-start) | collective-permute-done | bytes 1572896 | tf_op jit(solution)/shard_map/ppermute | solution.py:14
  12.9 0.1 constant_dynamic-update-slice_fusion
  13.0 0.0 copy-start
  13.0 1.6 copy-done
  14.6 0.0 copy-done.1
  14.6 4.9 %convolution_bitcast_fusion = f32[768,1535]{0,1:T(8,128)} fusion(bf16[1024,768]{1,0:T(8,128)(2,1)S(1)} %copy-done.1, bf16[1024,1536]{1,0:T(8,128)(2,1)S(1)} %constant_dynamic-update-slice_fusion), kind=kOutput, calls=%fused_computation.11 | convolution fusion | flops 2414346240 | bytes 9434112 | tf_op jit(solution)/shard_map/dot_general | solution.py:33
  19.6 6.1 %copy.8 = f32[768,1535]{1,0:T(8,128)} copy(f32[768,1535]{0,1:T(8,128)} %convolution_bitcast_fusion) | data formatting | bytes 9431040 | tf_op jit(solution)/shard_map/dot_general | solution.py:33
  25.6 7.8 %reshape.30 = f32[1178880]{0:T(1024)} reshape(f32[768,1535]{1,0:T(8,128)} %copy.8) | data formatting | bytes 9431040 | tf_op jit(solution)/shard_map/reshape | solution.py:19
  33.5 4.1 %pad.19 = f32[1179648]{0:T(1024)} pad(f32[1178880]{0:T(1024)} %reshape.30, f32[]{:T(128)} %constant.12.clone.1), padding=0_768 | pad | bytes 9434116 | tf_op jit(solution)/shard_map/jit(_pad)/pad | solution.py:19
  37.6 5.8 %reshape.31 = f32[768,1536]{1,0:T(8,128)} reshape(f32[1179648]{0:T(1024)} %pad.19) | data formatting | bytes 9437184 | tf_op jit(solution)/shard_map/reshape | solution.py:20
  43.4 0.0 copy-start.3
  43.4 0.0 copy-start.5
  43.4 0.0 copy-start.4
  43.4 3.3 %slice.21 = f32[768,768]{1,0:T(8,128)} slice(f32[768,1536]{1,0:T(8,128)} %reshape.31), slice={[0:768], [0:768]} | slice | bytes 4718592 | tf_op jit(solution)/shard_map/slice | solution.py:20
  46.7 0.0 all-reduce.8.cloned.1.call-update
  46.7 0.0 copy-done.3
  46.8 0.0 copy-done.5
  46.8 0.1 dynamic_slice.26
  46.9 0.0 copy-done.4
  46.9 0.1 pad_dynamic-slice_fusion.4
  47.0 0.1 pad_dynamic-slice_fusion.5
  47.0 2.8 %convert_reduce_fusion = (f32[1536]{0:T(1024)S(1)}, f32[1536]{0:T(1024)S(1)}) fusion(bf16[1024,1536]{1,0:T(8,128)(2,1)} %copy-done), kind=kLoop, calls=%fused_computation.1 | loop fusion | flops 6288384 | bytes 3158016 | tf_op jit(solution)/shard_map/reduce_sum | solution.py:91
  49.8 40.4 %all-reduce.5 = (f32[1536]{0:T(1024)S(1)}, f32[1536]{0:T(1024)S(1)}) all-reduce(f32[1536]{0:T(1024)S(1)} %get-tuple-element.3, f32[1536]{0:T(1024)S(1)} %get-tuple-element.2), channel_id=1, replica_groups=mesh['groups'=2,'samples'=8,'genome'=2] {'samples'}, use_global_device_ids=true, to_apply=%region_4.5 | all-reduce | flops 3072 | bytes 24576 | tf_op jit(solution)/shard_map/psum | solution.py:90
  90.2 68.7 %all-reduce.8.cloned.1.call-done = f32[768,768]{1,0:T(8,128)} async-done(((f32[768,768]{1,0:T(8,128)}), f32[768,768]{1,0:T(8,128)}) %all-reduce.8.cloned.1.call-update) | async-done | bytes 2359312 | tf_op jit(solution)/shard_map/psum | solution.py:101
  158.9 4.8 %pad.20 = f32[768,1537]{1,0:T(8,128)} pad(f32[768,768]{1,0:T(8,128)} %all-reduce.8.cloned.1.call-done, f32[]{:T(128)} %constant.12.clone.1), padding=0_0x1_768 | pad | bytes 7080964 | tf_op jit(solution)/shard_map/jit(_pad)/pad | solution.py:26
  163.7 8.1 %reshape.32 = f32[1180416]{0:T(1024)} reshape(f32[768,1537]{1,0:T(8,128)} %pad.20) | data formatting | bytes 9443328 | tf_op jit(solution)/shard_map/reshape | solution.py:27
  171.8 3.9 %slice_multiply_fusion = f32[1179648]{0:T(1024)} fusion(f32[1180416]{0:T(1024)} %reshape.32), kind=kLoop, calls=%fused_computation.3 | loop fusion | flops 1179648 | bytes 9437184 | tf_op jit(solution)/shard_map/div | solution.py:57
  175.8 5.8 %div.25 = f32[768,1536]{1,0:T(8,128)} reshape(f32[1179648]{0:T(1024)} %slice_multiply_fusion) | data formatting | bytes 9437184 | tf_op jit(solution)/shard_map/div | solution.py:57
  181.6 5.4 %subtract_select_fusion = f32[768,1536]{1,0:T(8,128)S(1)} fusion(f32[768,1536]{1,0:T(8,128)} %div.25, f32[1536]{0:T(1024)S(1)} %get-tuple-element.7, f32[768]{0:T(1024)S(1)} %dynamic_slice.35, f32[1536]{0:T(1024)S(1)} %get-tuple-element.6, f32[768]{0:T(1024)S(1)} %dynamic_slice.34, s32[1536]{0:T(1024)S(1)} %pad_dynamic-slice_fusion.5, ...), kind=kLoop, calls=%fused_computation.4 | loop fusion | flops 18874368 | bytes 9469440 | tf_op jit(solution)/shard_map/jit(_where)/select_n | solution.py:70
  187.1 4.7 %fusion.7 = f32[97,768]{1,0:T(8,128)S(1)} fusion(f32[768,1536]{1,0:T(8,128)S(1)} %subtract_select_fusion, s32[]{:T(128)S(6)} %select_n.12, f32[97,1536]{1,0:T(8,128)S(1)} %convert_element_type.17), kind=kOutput, calls=%fused_computation.17 | convolution fusion | flops 1373110272 | bytes 5612548 | tf_op jit(solution)/shard_map/dot_general | solution.py:72
  191.8 0.0 copy-start.6
  191.8 2.7 %convolution_add_fusion = f32[97,1536]{1,0:T(8,128)S(1)} fusion(f32[768,1536]{1,0:T(8,128)S(1)} %subtract_select_fusion, f32[97,768]{1,0:T(8,128)S(1)} %fusion.7, s32[]{:T(128)S(6)} %select_n.12, f32[97,1536]{1,0:T(8,128)S(1)} %convert_element_type.17), kind=kOutput, calls=%fused_computation.13 | convolution fusion | flops 1373259264 | bytes 6208516 | tf_op jit(solution)/shard_map/dot_general | solution.py:75
  194.5 1.3 collective-permute-start.1
  195.9 0.0 copy-done.6
  195.9 0.1 dynamic_slice.32
  195.9 0.9 collective-permute-done.1
  196.9 0.1 fusion.8
  196.9 0.0 copy-start.2
  196.9 0.4 convolution_bitcast_fusion.1
  197.4 2.0 all-gather.1
  199.3 0.7 reduce_sum.29
  200.0 0.0 copy-done.2
  (6 shorter events, 0.1 us)
Async XLA Ops:
  7.2 7.5 %copy-start.1 = (bf16[1024,768]{1,0:T(8,128)(2,1)S(1)}, bf16[1024,768]{1,0:T(8,128)(2,1)}, u32[]{:S(2)}) copy-start(bf16[1024,768]{1,0:T(8,128)(2,1)} %param.5) | copy-start | bytes 4718596
  7.2 151.7 %all-reduce.8.cloned.1.call-start = ((), (), s32[]{:S(2)}) async-start(), calls=%async_computation | async-start | bytes 4718592 | tf_op jit(solution)/shard_map/psum | solution.py:101
  7.2 5.6 %collective-permute-start = (bf16[1024,768]{1,0:T(8,128)(2,1)}, bf16[1024,768]{1,0:T(8,128)(2,1)S(1)}, u32[]{:S(2)}, u32[]{:S(2)}) collective-permute-start(bf16[1024,768]{1,0:T(8,128)(2,1)} %param.5), channel_id=1, source_target_pairs={{1,0},{3,2},{5,4},{7,6},{9,8},{11,10},{13,12},{15,14},{17,16},{19,... | collective-permute-start | bytes 4718600 | tf_op jit(solution)/shard_map/ppermute | solution.py:14
  13.0 1.6 copy-start
  43.4 3.3 %copy-start.3 = (s32[97,1536]{1,0:T(8,128)S(1)}, s32[97,1536]{1,0:T(8,128)}, u32[]{:S(2)}) copy-start(s32[97,1536]{1,0:T(8,128)} %param.8) | copy-start | bytes 1787908
  43.4 3.4 %copy-start.5 = (s32[1536]{0:T(1024)S(1)}, s32[1536]{0:T(1024)}, u32[]{:S(2)}) copy-start(s32[1536]{0:T(1024)} %param.9) | copy-start | bytes 18436
  43.4 3.5 %copy-start.4 = (s32[1536]{0:T(1024)S(1)}, s32[1536]{0:T(1024)}, u32[]{:S(2)}) copy-start(s32[1536]{0:T(1024)} %param.6) | copy-start | bytes 18436
  191.8 4.1 %copy-start.6 = (s32[1536]{0:T(1024)S(1)}, s32[1536]{0:T(1024)}, u32[]{:S(2)}) copy-start(s32[1536]{0:T(1024)} %param.7) | copy-start | bytes 18436
  194.5 2.3 %collective-permute-start.1 = (bf16[97,768]{1,0:T(8,128)(2,1)S(1)}, bf16[97,768]{1,0:T(8,128)(2,1)S(1)}, u32[]{:S(2)}, u32[]{:S(2)}) collective-permute-start(bf16[97,768]{1,0:T(8,128)(2,1)S(1)} %slice.30), channel_id=1, source_target_pairs={{0,1},{2,3},{4,5},{6,7},{8,9},{10,11},{12,13},{14,15},{16,17},{18,... | collective-permute-start | bytes 446984 | tf_op jit(solution)/shard_map/ppermute | solution.py:14
  196.9 3.1 %copy-start.2 = (f32[97,768]{1,0:T(8,128)}, f32[97,768]{1,0:T(8,128)S(1)}, u32[]{:S(2)}) copy-start(f32[97,768]{1,0:T(8,128)S(1)} %fusion.8) | copy-start | bytes 893956
Sparse Core Ops, SparseCore 0:
  46.8 112.0 all-reduce.7
